TPU v7x, 128 devices: a whole 4x4x4 slice. The times are simulated.
128 devices in a mesh: chan: 8 (over y, core), facet: 16 (over z, x).
Axes of the slice: x: 4, y: 4, z: 4, core: 2. Of those that a mesh axis runs over, the one named last changes fastest.
Arguments:
- visibilities: bfloat16 [32, 8, 8, 65536], P(None, None, 'chan', 'facet'), may hold values from -6 to 6
- w_kernel: bfloat16 [32, 2, 8], replicated, may hold values from -2 to 2
- w_index: int32 [8, 65536], P(None, 'facet'), may hold values from 0 to 31
- cell_offsets: int32 [2, 8, 65536], P(None, None, 'facet'), may hold values from 0 to 24
- block_sub: int32 [8, 128], P(None, 'facet'), may hold values from 0 to 31
- intersection_rows: int32 [16, 32], replicated, may hold values from 0 to 63, as said below
- intersection_count: int32 [16], replicated, may hold values from 1 to 32, as said below
Outputs:
- sky_image: float32 [32, 4, 64, 32768], P('chan', None, None, 'facet')
Inputs may be any that keep to these rules, and one draw needn't show every extreme that they name: `intersection_rows`: the rows in one facet's list are distinct. `intersection_count`: some facet other than the last has exactly 32 entries in use.
All inputs are finite; a program needn't handle non-finite values.
Results may differ from a plain program's by a relative error of at most 0.0059.
Values may be sent and summed in bfloat16 or wider, within the bound.
A program may use at most 128 MiB of HBM per device.

v0:
```python
import math
import jax
import jax.numpy as jnp
from jax import lax
from jax.sharding import PartitionSpec as P

BLK = 512
SG = 32
NSUB = 32
FX = 2048
FY = 64
MARGIN = 128


def shifted(block, axis, distance):
    devices = range(lax.axis_size(axis))
    route = [(i - distance, i) for i in devices if i - distance in devices]
    return lax.ppermute(block, axis, route)


def anchors(sub_index, side_len, period):
    span = period // side_len
    row_anchor = (jnp.mod(sub_index * 37, span) - span // 2) * side_len
    col_anchor = (jnp.mod(sub_index * 53 + 5, span) - span // 2) * side_len
    return (row_anchor, col_anchor)


def row_tables(sub_index, side_len, height, period):
    row_anchor, col_anchor = anchors(sub_index, side_len, period)
    cell_ids = jnp.arange(side_len, dtype=jnp.int32)
    line_ids = jnp.arange(height, dtype=jnp.int32) - height // 2
    phase_int = (row_anchor[:, None, None] + cell_ids[None, None, :]) * line_ids[None, :, None]
    radians = jnp.mod(phase_int, period).astype(jnp.float32) * (2.0 * math.pi / period)
    return (jnp.cos(radians).astype(jnp.bfloat16), jnp.sin(radians).astype(jnp.bfloat16))


def col_tables(sub_index, side_len, col_ids, period):
    row_anchor, col_anchor = anchors(sub_index, side_len, period)
    cell_ids = jnp.arange(side_len, dtype=jnp.int32)
    phase_int = (col_anchor[:, None, None] + cell_ids[None, :, None]) * (col_ids - period // 2)[
        None, None, :
    ]
    radians = jnp.mod(phase_int, period).astype(jnp.float32) * (2.0 * math.pi / period)
    return (jnp.cos(radians).astype(jnp.bfloat16), (-jnp.sin(radians)).astype(jnp.bfloat16))


def place_kernel(values, offsets, side_len):
    distance = jnp.arange(side_len, dtype=jnp.int32)[:, None] - offsets[None, :]
    running = jnp.zeros((values.shape[0], side_len, offsets.shape[0]), jnp.float32)
    for tap_idx in range(values.shape[1]):
        running = (
            running + values[:, tap_idx, None, :] * (distance == tap_idx).astype(jnp.float32)[None]
        )
    return running


def combine(products, side_len, row_width):
    real_part = products[:, :side_len, :row_width] - products[:, side_len:, row_width:]
    imag_part = products[:, :side_len, row_width:] + products[:, side_len:, :row_width]
    return jnp.stack([real_part, imag_part], axis=1)


def block_terms(vis_part, plane_ids, cell_pos, kernel, side_len, block_len):
    planes = kernel.shape[0]
    plane_pick = (jnp.arange(planes, dtype=jnp.int32)[:, None] == plane_ids[None, :]).astype(
        jnp.float32
    )
    values = jnp.einsum(
        "wqk,wr->qkr", kernel.astype(jnp.float32), plane_pick, precision=lax.Precision.HIGHEST
    )
    left_kern = place_kernel(values, cell_pos[0], side_len).astype(jnp.bfloat16)
    right_kern = place_kernel(values, cell_pos[1], side_len)
    num_pols = vis_part.shape[1] // 2
    vis_real = vis_part[:, :num_pols].astype(jnp.float32)[:, :, None, :]
    vis_imag = vis_part[:, num_pols:].astype(jnp.float32)[:, :, None, :]
    y_real = (vis_real * right_kern[0][None, None] - vis_imag * right_kern[1][None, None]).astype(
        jnp.bfloat16
    )
    y_imag = (vis_real * right_kern[1][None, None] + vis_imag * right_kern[0][None, None]).astype(
        jnp.bfloat16
    )
    num_rows = plane_ids.shape[0]
    blocks = num_rows // block_len
    row_width = vis_part.shape[0] * num_pols * side_len
    stacked = jnp.concatenate(
        [
            y_real.reshape(row_width, blocks, block_len),
            y_imag.reshape(row_width, blocks, block_len),
        ],
        axis=0,
    )
    left_flat = left_kern.reshape(2 * side_len, blocks, block_len)
    products = lax.dot_general(
        left_flat, stacked, (((2,), (2,)), ((1,), (1,))), preferred_element_type=jnp.float32
    )
    return combine(products, side_len, row_width)


def to_rows(subgrid, row_cos, row_sin, img_scale):
    sub_real = subgrid[:, 0]
    sub_imag = subgrid[:, 1]

    def apply_table(table, data):
        return jnp.einsum("gyu,guq->gyq", table, data, preferred_element_type=jnp.float32)

    real_part = apply_table(row_cos, sub_real) - apply_table(row_sin, sub_imag)
    imag_part = apply_table(row_cos, sub_imag) + apply_table(row_sin, sub_real)
    return (jnp.stack([real_part, imag_part], axis=1) * img_scale).astype(jnp.bfloat16)


def project(image_sum, row_image, first_sub, col_ids, period):
    num_items = row_image.shape[0]
    group_len = math.gcd(num_items, 8)
    side_len = SG
    mixed = image_sum.shape[0]
    shaped = row_image.reshape(num_items, 2, row_image.shape[2], mixed, side_len)

    def add_group(turn_idx, running):
        row_piece = lax.dynamic_slice_in_dim(shaped, turn_idx * group_len, group_len, 0)
        sub_index = first_sub + turn_idx * group_len + jnp.arange(group_len, dtype=jnp.int32)
        col_cos, col_sin = col_tables(sub_index, side_len, col_ids, period)
        col_table = jnp.stack([col_cos, col_sin], axis=1)
        return running + jnp.einsum(
            "grycv,grvx->cyx", row_piece, col_table, preferred_element_type=jnp.float32
        )

    return lax.fori_loop(0, num_items // group_len, add_group, image_sum)


def shards(
    visibilities, w_kernel, w_index, cell_offsets, block_sub, intersection_rows, intersection_count
):
    turned = lax.all_to_all(visibilities, "chan", split_axis=0, concat_axis=2, tiled=True)
    groups = lax.axis_size("chan")
    facets = lax.axis_size("facet")
    num_chans = turned.shape[0]
    num_pols = turned.shape[1] // 2
    side_len = SG
    per_dev = w_index.shape[1] // BLK
    row_width = num_chans * num_pols * side_len

    def grid_group(group_id):
        vis_part = lax.dynamic_index_in_dim(turned, group_id, 2, keepdims=False)
        plane_ids = lax.dynamic_index_in_dim(w_index, group_id, 0, keepdims=False)
        cell_pos = lax.dynamic_index_in_dim(cell_offsets, group_id, 1, keepdims=False)
        return block_terms(vis_part, plane_ids, cell_pos, w_kernel, side_len, BLK)

    grid_parts = lax.map(grid_group, jnp.arange(groups, dtype=jnp.int32))
    blocks = groups * per_dev
    grid_parts = grid_parts.reshape(blocks, 2 * side_len * row_width)
    sub_ids = block_sub.reshape(blocks)
    plane_pick = (jnp.arange(NSUB, dtype=jnp.int32)[:, None] == sub_ids[None, :]).astype(
        jnp.float32
    )
    img_scale = 1.0 / math.sqrt(groups * facets * w_index.shape[1])
    period = FX * facets
    facet_id = lax.axis_index("facet")
    col_ids = facet_id * FX + jnp.arange(FX, dtype=jnp.int32)
    image = jnp.zeros((num_chans * num_pols, FY, FX), jnp.float32)
    partial_sum = jnp.dot(plane_pick, grid_parts, precision=lax.Precision.HIGHEST)
    summed = lax.psum(partial_sum, "facet")
    subgrid = summed.reshape(NSUB, 2, side_len, row_width).astype(jnp.bfloat16)
    sub_index = jnp.arange(NSUB, dtype=jnp.int32)
    row_cos, row_sin = row_tables(sub_index, side_len, FY, period)
    row_image = to_rows(subgrid, row_cos, row_sin, img_scale)
    image = project(image, row_image, 0, col_ids, period)
    line_ids = jnp.arange(FY, dtype=jnp.int32)
    slot_ids = jnp.arange(intersection_rows.shape[1], dtype=jnp.int32)
    edge_cols = image[:, :, FX - MARGIN :]
    listed = lax.dynamic_index_in_dim(intersection_rows, facet_id, 0, keepdims=False)
    in_use = lax.dynamic_index_in_dim(intersection_count, facet_id, 0, keepdims=False)
    row_keep = jnp.sum(
        ((listed[:, None] == line_ids[None, :]) & (slot_ids[:, None] < in_use)).astype(jnp.float32),
        axis=0,
    )
    arrived = shifted(edge_cols * row_keep[None, :, None], "facet", 1)
    sky_image = jnp.concatenate([image[:, :, :MARGIN] + arrived, image[:, :, MARGIN:]], axis=2)
    return sky_image.reshape(num_chans, num_pols, FY, FX)


def solution(mesh):
    return jax.shard_map(
        shards,
        mesh=mesh,
        in_specs=(
            P(None, None, "chan", "facet"),
            P(),
            P(None, "facet"),
            P(None, None, "facet"),
            P(None, "facet"),
            P(),
            P(),
        ),
        out_specs=P("chan", None, None, "facet"),
        check_vma=False,
    )
```

profile of v0, /device:TPU:2, one launch (start us, length us, event | category | flops | bytes accessed | tf_op | source)
XLA Modules:
  0.0 462.6 jit_solution(6023699204950626542)
XLA Ops:
  0.0 4.6 all-to-all-start
  6.7 25.1 %all-to-all-done = bf16[32,8,1,4096]{3,1,2,0:T(8,128)(2,1)S(1)} async-done(((bf16[32,8,1,4096]{3,1,2,0:T(8,128)(2,1)}), bf16[32,8,1,4096]{3,1,2,0:T(8,128)(2,1)S(1)}, u32[]{:S(2)}, u32[]{:S(2)}) %all-to-all-start) | async-done | bytes 2097184 | tf_op jit(solution)/shard_map/all_to_all | solution.py:133
  31.8 175.5 %while.27 = (s32[]{:T(128)}, f32[8,8,2,32,512]{4,3,2,1,0:T(8,128)}, s32[8]{0:T(128)S(1)}, s32[8,4096]{1,0:T(8,128)}, bf16[32,2,8]{0,2,1:T(8,128)(2,1)S(1)}, /*in...) while((s32[]{:T(128)}, f32[8,8,2,32,512]{4,3,2,1,0:T(8,128)}, ...), condition=%wide.region_1.2_spmd, body=%wide.region_0.1_spmd.sunk | while | flops 587988992 | bytes 84559040 | solution.py:148
  39.4 2.6 subtract_convert_fusion.2
  42.0 2.2 copy.91
  44.3 1.5 copy.92
  45.7 2.2 copy.93
  48.0 1.5 copy.94
  49.4 3.0 fusion.100
  61.3 2.6 subtract_convert_fusion.2
  63.9 2.2 copy.91
  66.2 1.5 copy.92
  67.6 2.2 copy.93
  69.9 1.5 copy.94
  71.3 3.0 fusion.100
  83.3 2.6 subtract_convert_fusion.2
  85.9 2.2 copy.91
  88.1 1.5 copy.92
  89.6 2.2 copy.93
  93.3 3.0 fusion.100
  105.2 2.6 subtract_convert_fusion.2
  107.8 2.2 copy.91
  111.5 2.2 copy.93
  115.2 3.0 fusion.100
  127.1 2.6 subtract_convert_fusion.2
  129.8 2.2 copy.91
  133.5 2.2 copy.93
  137.2 3.0 fusion.100
  149.1 2.6 subtract_convert_fusion.2
  151.7 2.2 copy.91
  155.4 2.2 copy.93
  159.1 3.0 fusion.100
  171.0 2.6 subtract_convert_fusion.2
  173.6 2.2 copy.91
  177.3 2.2 copy.93
  181.0 3.0 fusion.100
  192.9 2.6 subtract_convert_fusion.2
  195.6 2.2 copy.91
  199.3 2.2 copy.93
  203.0 3.0 fusion.100
  207.4 9.4 %reshape.590 = f32[64,32768]{1,0:T(8,128)} reshape(f32[8,8,2,32,512]{4,3,2,1,0:T(8,128)} %get-tuple-element.178) | data formatting | bytes 16777216 | tf_op jit(solution)/shard_map/reshape | solution.py:150
  216.7 8.4 %fusion.60 = f32[32,32768]{1,0:T(8,128)} fusion(f32[64,32768]{1,0:T(8,128)} %reshape.590, s32[64]{0:T(128)S(1)} %eq.182), kind=kOutput, calls=%fused_computation.121 | convolution fusion | flops 805308416 | bytes 12583168 | tf_op jit(solution)/shard_map/dot_general | solution.py:160
  225.1 103.7 %all-reduce.1 = bf16[32,32768]{1,0:T(8,128)(2,1)} all-reduce(f32[32,32768]{1,0:T(8,128)} %fusion.60), channel_id=1, replica_groups=mesh['chan'=8,'facet'=16] {'facet'}, use_global_device_ids=true, to_apply=%region_2.3 | all-reduce | flops 1048576 | bytes 6291456 | tf_op jit(solution)/shard_map/psum | solution.py:161
  328.8 2.3 copy.59
  331.1 2.7 fusion.56
  333.9 4.1 fusion.55
  337.9 4.2 convolution_add_fusion
  342.1 6.8 %copy.38 = f32[32,64,512]{1,2,0:T(8,128)} copy(f32[32,64,512]{2,1,0:T(8,128)} %convolution_add_fusion) | data formatting | bytes 8388608 | tf_op jit(solution)/shard_map/add | solution.py:107
  349.0 5.7 %convolution_subtract_fusion = f32[32,64,512]{2,1,0:T(8,128)} fusion(f32[32,64,512]{2,1,0:T(8,128)} %fusion.55, bf16[32,2,32,512]{3,2,1,0:T(8,128)(2,1)S(1)} %bitcast.145, s32[64]{0:T(128)S(1)} %iota_add_fusion.2, s32[32,32]{1,0:T(8,128)S(1)} %iota_add_fusion.1), kind=kOutput, calls=%fused_computation.100 | convolution fusion | flops 69140480 | bytes 9454080 | tf_op jit(solution)/shard_map/gyu,guq->gyq/dot_general | solution.py:104
  354.7 6.9 %copy.37 = f32[32,64,512]{1,2,0:T(8,128)} copy(f32[32,64,512]{2,1,0:T(8,128)} %convolution_subtract_fusion) | data formatting | bytes 8388608 | tf_op jit(solution)/shard_map/sub | solution.py:106
  361.6 9.8 %fusion.54 = bf16[32,2,64,16,32]{2,4,3,0,1:T(8,128)(2,1)} fusion(f32[32,1,64,16,32]{2,4,3,0,1:T(8,128)} %bitcast.140, f32[32,1,64,16,32]{2,4,3,0,1:T(8,128)} %bitcast.141), kind=kLoop, calls=%fused_computation.97 | loop fusion | flops 6291456 | bytes 12582912 | tf_op jit(solution)/shard_map/convert_element_type | solution.py:108
  371.5 73.2 %while.28 = (s32[]{:T(128)}, f32[16,64,2048]{2,1,0:T(8,128)}, bf16[32,2,64,16,32]{2,4,3,0,1:T(8,128)(2,1)}, s32[]{:T(128)}, s32[]{:T(128)}, /*index=5*/s32[]{:T(128)}, s32[]{:T(128)}, s32[]{:T(128)}) while((s32[]{:T(128)}, f32[16,64,2048]{2,1,0:T(8,128)}, bf16[32,2,64,16,32]{2,4,3,0,1:T(8,128)(2,1)}, s32[]{:T(128)}, s32[]{:T(128)}, ...), condition=%wide.region_4.5_spmd.clone, body=%wide.region_3.4_spmd.clone.sunk | while | flops 2164789760 | bytes 23087328 | solution.py:127
  371.5 8.9 %cosine_convert_fusion.5 = (bf16[8,1,32,2048]{3,2,1,0:T(8,128)(2,1)S(1)}, bf16[8,1,32,2048]{3,2,1,0:T(8,128)(2,1)S(1)}) fusion(s32[2048]{0:T(1024)S(1)} %add_add_fusion.2, s32[8,32]{1,0:T(8,128)S(1)} %iota_add_fusion.4), kind=kLoop, calls=%fused_computation.85.clone.1 | loop fusion | flops 8912896 | bytes 2106368 | tf_op jit(solution)/shard_map/while/body/eval_jaxpr/convert_element_type | solution.py:44
  380.5 7.4 %bitcast_add_fusion.2 = f32[16,64,2048]{2,1,0:T(8,128)} fusion(f32[16,64,2048]{2,1,0:T(8,128)} %get-tuple-element.474, pred[]{:T(512)S(6)} %compare.19, bf16[8,1,32,2048]{3,2,1,0:T(8,128)(2,1)S(1)} %get-tuple-element.430, bf16[8,1,32,2048]{3,2,1,0:T(8,128)(2,1)S(1)} %get-tuple-element.431, bf16[32,2,64,16,32]{2,4,3,0,1:T(8,128)(2,1)} %get-tuple-element.483, ...), kind=kOutput, calls=%fused_computation.71.clone.1 | convolution fusion | flops 2155872256 | bytes 20971524 | tf_op jit(solution)/shard_map/while/body/eval_jaxpr/grycv,grvx->cyx/dot_general | solution.py:123
  388.0 8.9 %cosine_convert_fusion.5 = (bf16[8,1,32,2048]{3,2,1,0:T(8,128)(2,1)S(1)}, bf16[8,1,32,2048]{3,2,1,0:T(8,128)(2,1)S(1)}) fusion(s32[2048]{0:T(1024)S(1)} %add_add_fusion.2, s32[8,32]{1,0:T(8,128)S(1)} %iota_add_fusion.4), kind=kLoop, calls=%fused_computation.85.clone.1 | loop fusion | flops 8912896 | bytes 2106368 | tf_op jit(solution)/shard_map/while/body/eval_jaxpr/convert_element_type | solution.py:44
  397.0 9.9 %bitcast_add_fusion.2 = f32[16,64,2048]{2,1,0:T(8,128)} fusion(f32[16,64,2048]{2,1,0:T(8,128)} %get-tuple-element.474, pred[]{:T(512)S(6)} %compare.19, bf16[8,1,32,2048]{3,2,1,0:T(8,128)(2,1)S(1)} %get-tuple-element.430, bf16[8,1,32,2048]{3,2,1,0:T(8,128)(2,1)S(1)} %get-tuple-element.431, bf16[32,2,64,16,32]{2,4,3,0,1:T(8,128)(2,1)} %get-tuple-element.483, ...), kind=kOutput, calls=%fused_computation.71.clone.1 | convolution fusion | flops 2155872256 | bytes 20971524 | tf_op jit(solution)/shard_map/while/body/eval_jaxpr/grycv,grvx->cyx/dot_general | solution.py:123
  406.9 8.9 %cosine_convert_fusion.5 = (bf16[8,1,32,2048]{3,2,1,0:T(8,128)(2,1)S(1)}, bf16[8,1,32,2048]{3,2,1,0:T(8,128)(2,1)S(1)}) fusion(s32[2048]{0:T(1024)S(1)} %add_add_fusion.2, s32[8,32]{1,0:T(8,128)S(1)} %iota_add_fusion.4), kind=kLoop, calls=%fused_computation.85.clone.1 | loop fusion | flops 8912896 | bytes 2106368 | tf_op jit(solution)/shard_map/while/body/eval_jaxpr/convert_element_type | solution.py:44
  415.9 9.9 %bitcast_add_fusion.2 = f32[16,64,2048]{2,1,0:T(8,128)} fusion(f32[16,64,2048]{2,1,0:T(8,128)} %get-tuple-element.474, pred[]{:T(512)S(6)} %compare.19, bf16[8,1,32,2048]{3,2,1,0:T(8,128)(2,1)S(1)} %get-tuple-element.430, bf16[8,1,32,2048]{3,2,1,0:T(8,128)(2,1)S(1)} %get-tuple-element.431, bf16[32,2,64,16,32]{2,4,3,0,1:T(8,128)(2,1)} %get-tuple-element.483, ...), kind=kOutput, calls=%fused_computation.71.clone.1 | convolution fusion | flops 2155872256 | bytes 20971524 | tf_op jit(solution)/shard_map/while/body/eval_jaxpr/grycv,grvx->cyx/dot_general | solution.py:123
  425.8 8.9 %cosine_convert_fusion.5 = (bf16[8,1,32,2048]{3,2,1,0:T(8,128)(2,1)S(1)}, bf16[8,1,32,2048]{3,2,1,0:T(8,128)(2,1)S(1)}) fusion(s32[2048]{0:T(1024)S(1)} %add_add_fusion.2, s32[8,32]{1,0:T(8,128)S(1)} %iota_add_fusion.4), kind=kLoop, calls=%fused_computation.85.clone.1 | loop fusion | flops 8912896 | bytes 2106368 | tf_op jit(solution)/shard_map/while/body/eval_jaxpr/convert_element_type | solution.py:44
  434.8 9.9 %bitcast_add_fusion.2 = f32[16,64,2048]{2,1,0:T(8,128)} fusion(f32[16,64,2048]{2,1,0:T(8,128)} %get-tuple-element.474, pred[]{:T(512)S(6)} %compare.19, bf16[8,1,32,2048]{3,2,1,0:T(8,128)(2,1)S(1)} %get-tuple-element.430, bf16[8,1,32,2048]{3,2,1,0:T(8,128)(2,1)S(1)} %get-tuple-element.431, bf16[32,2,64,16,32]{2,4,3,0,1:T(8,128)(2,1)} %get-tuple-element.483, ...), kind=kOutput, calls=%fused_computation.71.clone.1 | convolution fusion | flops 2155872256 | bytes 20971524 | tf_op jit(solution)/shard_map/while/body/eval_jaxpr/grycv,grvx->cyx/dot_general | solution.py:123
  445.8 1.9 collective-permute-start
  447.7 3.8 slice.85
  451.5 5.3 %collective-permute-done = f32[16,64,128]{2,1,0:T(8,128)S(1)} collective-permute-done((f32[16,64,128]{2,1,0:T(8,128)S(1)}, f32[16,64,128]{2,1,0:T(8,128)S(1)}, u32[]{:S(2)}, u32[]{:S(2)}) %collective-permute-start) | collective-permute-done | bytes 524320 | tf_op jit(solution)/shard_map/ppermute | solution.py:18
  458.0 4.6 pad_maximum_fusion
  (200 shorter events, 75.5 us)
Async XLA Ops:
  0.0 6.0 %copy-start = (s32[16,32]{1,0:T(8,128)S(1)}, s32[16,32]{1,0:T(8,128)}, u32[]{:S(2)}) copy-start(s32[16,32]{1,0:T(8,128)} %param.16) | copy-start | bytes 6148
  0.0 4.6 %copy-start.3 = (s32[8,8]{1,0:T(8,128)S(1)}, s32[8,8]{1,0:T(8,128)}, u32[]{:S(2)}) copy-start(s32[8,8]{1,0:T(8,128)} %param.15) | copy-start | bytes 772
  0.0 4.7 %copy-start.5 = (s32[16]{0:T(128)S(1)}, s32[16]{0:T(128)}, u32[]{:S(2)}) copy-start(s32[16]{0:T(128)} %param.17) | copy-start | bytes 196
  0.0 31.8 %copy-start.2 = (bf16[32,2,8]{0,2,1:T(8,128)(2,1)S(1)}, bf16[32,2,8]{0,2,1:T(8,128)(2,1)}, u32[]{:S(2)}) copy-start(bf16[32,2,8]{0,2,1:T(8,128)(2,1)} %param.12) | copy-start | bytes 3076
  0.0 31.8 %all-to-all-start = ((bf16[32,8,1,4096]{3,1,2,0:T(8,128)(2,1)}), bf16[32,8,1,4096]{3,1,2,0:T(8,128)(2,1)S(1)}, u32[]{:S(2)}, u32[]{:S(2)}) async-start(bf16[32,8,1,4096]{3,1,2,0:T(8,128)(2,1)} %param.11), calls=%async_computation | async-start | bytes 4194304 | tf_op jit(solution)/shard_map/all_to_all | solution.py:133
  371.5 73.2 %copy-start.4 = (f32[64]{0:T(128)S(1)}, f32[64]{0:T(128)}, u32[]{:S(2)}) copy-start(f32[64]{0:T(128)} %convert_reduce_fusion) | copy-start | bytes 772
  445.8 11.1 %collective-permute-start = (f32[16,64,128]{2,1,0:T(8,128)S(1)}, f32[16,64,128]{2,1,0:T(8,128)S(1)}, u32[]{:S(2)}, u32[]{:S(2)}) collective-permute-start(f32[16,64,128]{2,1,0:T(8,128)S(1)} %slice_multiply_fusion), channel_id=1, source_target_pairs={{0,1},{1,2},{2,3},{3,4},{4,5},{5,6},{6,7},{7,8},{8,9},{9,10},{10,1... | collective-permute-start | bytes 1572872 | tf_op jit(solution)/shard_map/ppermute | solution.py:18
  458.0 4.6 copy-start.1
where the time goes:
time: 464 us; the launch traced here: 463 us
  local copies, waits for them, and re-layouts  115 us (25%)
  blocking collectives  104 us (22%)
  other arithmetic  102 us (22%)
  matrix products  88.1 us (19%)
  waiting for transfers between devices  30.5 us (7%)
  loops' own time  16.5 us (4%)
  starting transfers between devices  6.53 us (1%)
    psum x1, blocking collectives, shards(): summed = lax.psum(partial_sum, 'facet')  104 us
    while x56, local copies, waits for them, and re-layouts  38.8 us
    dot_general x4, matrix products, add_group(): jnp.einsum('grycv,grvx->cyx', row_piece, col_table, preferred_element_typ...  37.1 us
    convert_element_type x4, other arithmetic, col_tables(): jnp.cos(radians).astype(jnp.bfloat16)  35.7 us
    all_to_all x1, waiting for transfers between devices, shards(): lax.all_to_all(visibilities, 'chan', split_axis=0, concat_axis=2, tiled=T...  25.1 us
    dot_general x8, matrix products, block_terms(): lax.dot_general(left_flat, stacked, (((2,), (2,)), ((1,), (1,))), preferr...  24.4 us
    convert_element_type x8, other arithmetic, block_terms(): (vis_real * right_kern[0][None, None] - vis_imag * right_kern[1][None, No...  21 us
    dot_general x4, matrix products, apply_table(): jnp.einsum('gyu,guq->gyq', table, data, preferred_element_type=jnp.float32)  16.7 us
  transfers between devices with their start and end apart: 2, of which 2 were waited for; matrix products, arithmetic and copies ran while one was open for 1% of the time, Pallas kernels for 0%

commit v1 on v0

--- a/solution.py
+++ b/solution.py
@@ -158,7 +158,7 @@
     col_ids = facet_id * FX + jnp.arange(FX, dtype=jnp.int32)
     image = jnp.zeros((num_chans * num_pols, FY, FX), jnp.float32)
     partial_sum = jnp.dot(plane_pick, grid_parts, precision=lax.Precision.HIGHEST)
-    summed = lax.psum(partial_sum, "facet")
+    summed = jnp.sum(lax.all_gather(partial_sum, "facet"), axis=0)
     subgrid = summed.reshape(NSUB, 2, side_len, row_width).astype(jnp.bfloat16)
     sub_index = jnp.arange(NSUB, dtype=jnp.int32)
     row_cos, row_sin = row_tables(sub_index, side_len, FY, period)

time: 464 us -> 773 us (1.67)
  waiting for transfers between devices: 30.5 us -> 403 us
  blocking collectives: 104 us -> 0 us
  other arithmetic: 102 us -> 124 us
  between operations: 0.11 us -> 13.5 us
    all_gather x0 -> x1, waiting for transfers between devices: none -> 367 us  [shards(): summed = jnp.sum(lax.all_gather(partial_sum, 'facet'), axis=0)]
    psum x1 -> x0, blocking collectives: 104 us -> none  [shards(): summed = lax.psum(partial_sum, 'facet')]
    reduce_sum x0 -> x1, other arithmetic: none -> 22.4 us  [shards(): summed = jnp.sum(lax.all_gather(partial_sum, 'facet'), axis=0)]
  transfers between devices with their start and end apart: 2 -> 3, of which waited for: 2 -> 3; matrix products, arithmetic and copies ran while one was open for 1% -> 1% of each run, Pallas kernels for 0% -> 0%
where the time goes in v1:
time: 773 us; the launch traced here: 770 us
  waiting for transfers between devices  403 us (52%)
  other arithmetic  124 us (16%)
  local copies, waits for them, and re-layouts  116 us (15%)
  matrix products  88.1 us (11%)
  loops' own time  17.9 us (2%)
  between operations  13.5 us (2%)
  starting transfers between devices  8.02 us (1%)
    all_gather x1, waiting for transfers between devices, shards(): summed = jnp.sum(lax.all_gather(partial_sum, 'facet'), axis=0)  367 us
    while x56, local copies, waits for them, and re-layouts  38.8 us
    dot_general x4, matrix products, add_group(): jnp.einsum('grycv,grvx->cyx', row_piece, col_table, preferred_element_typ...  37 us
    convert_element_type x4, other arithmetic, col_tables(): jnp.cos(radians).astype(jnp.bfloat16)  35.7 us
    all_to_all x1, waiting for transfers between devices, shards(): lax.all_to_all(visibilities, 'chan', split_axis=0, concat_axis=2, tiled=T...  27.1 us
    dot_general x8, matrix products, block_terms(): lax.dot_general(left_flat, stacked, (((2,), (2,)), ((1,), (1,))), preferr...  24.4 us
    reduce_sum x1, other arithmetic, shards(): summed = jnp.sum(lax.all_gather(partial_sum, 'facet'), axis=0)  22.4 us
    convert_element_type x8, other arithmetic, block_terms(): (vis_real * right_kern[0][None, None] - vis_imag * right_kern[1][None, No...  21 us
  transfers between devices with their start and end apart: 3, of which 3 were waited for; matrix products, arithmetic and copies ran while one was open for 1% of the time, Pallas kernels for 0%

profile of v1, /device:TPU:2, one launch (start us, length us, event | category | flops | bytes accessed | tf_op | source)
XLA Modules:
  0.0 770.2 jit_solution(5021690877551120553)
XLA Ops:
  6.5 4.6 all-to-all-start
  11.3 27.1 %all-to-all-done = bf16[32,8,1,4096]{3,1,2,0:T(8,128)(2,1)S(1)} async-done(((bf16[32,8,1,4096]{3,1,2,0:T(8,128)(2,1)}), bf16[32,8,1,4096]{3,1,2,0:T(8,128)(2,1)S(1)}, u32[]{:S(2)}, u32[]{:S(2)}) %all-to-all-start) | async-done | bytes 2097184 | tf_op jit(solution)/shard_map/all_to_all | solution.py:133
  38.4 177.2 %while.27 = (s32[]{:T(128)}, f32[8,8,2,32,512]{4,3,2,1,0:T(8,128)}, s32[8]{0:T(128)S(1)}, s32[8,4096]{1,0:T(8,128)}, bf16[32,2,8]{0,2,1:T(8,128)(2,1)S(1)}, /*in...) while((s32[]{:T(128)}, f32[8,8,2,32,512]{4,3,2,1,0:T(8,128)}, ...), condition=%wide.region_1.2_spmd, body=%wide.region_0.1_spmd.sunk | while | flops 587988992 | bytes 84559544 | solution.py:148
  46.1 2.6 subtract_convert_fusion.2
  48.8 2.2 copy.90
  51.0 1.5 copy.91
  52.5 2.2 copy.92
  54.7 1.5 copy.93
  56.2 3.0 fusion.100
  68.3 2.6 subtract_convert_fusion.2
  70.9 2.2 copy.90
  74.6 2.2 copy.92
  78.3 3.0 fusion.100
  90.4 2.6 subtract_convert_fusion.2
  93.1 2.2 copy.90
  96.8 2.2 copy.92
  100.4 3.0 fusion.100
  112.6 2.6 subtract_convert_fusion.2
  115.2 2.2 copy.90
  118.9 2.2 copy.92
  122.6 3.0 fusion.100
  134.7 2.6 subtract_convert_fusion.2
  137.3 2.2 copy.90
  139.6 1.5 copy.91
  141.0 2.2 copy.92
  144.7 3.0 fusion.100
  156.9 2.6 subtract_convert_fusion.2
  159.5 2.2 copy.90
  163.2 2.2 copy.92
  166.9 3.0 fusion.100
  179.0 2.6 subtract_convert_fusion.2
  181.6 2.2 copy.90
  185.3 2.2 copy.92
  189.0 3.0 fusion.100
  201.2 2.6 subtract_convert_fusion.2
  203.8 2.2 copy.90
  207.5 2.2 copy.92
  209.7 1.5 copy.93
  211.2 3.0 fusion.100
  215.5 9.4 %reshape.590 = f32[64,32768]{1,0:T(8,128)} reshape(f32[8,8,2,32,512]{4,3,2,1,0:T(8,128)} %get-tuple-element.178) | data formatting | bytes 16777216 | tf_op jit(solution)/shard_map/reshape | solution.py:150
  224.9 8.4 %fusion.60 = f32[32,32768]{1,0:T(8,128)} fusion(f32[64,32768]{1,0:T(8,128)} %reshape.590, s32[64]{0:T(128)S(1)} %eq.182), kind=kOutput, calls=%fused_computation.121 | convolution fusion | flops 805308416 | bytes 12583168 | tf_op jit(solution)/shard_map/dot_general | solution.py:160
  235.4 367.2 %all-gather.3.cloned.1.call-done = f32[512,32768]{1,0:T(8,128)} async-done(((f32[32,32768]{1,0:T(8,128)}), f32[512,32768]{1,0:T(8,128)}) %all-gather.3.cloned.1.call-update) | async-done | bytes 67108880 | tf_op jit(solution)/shard_map/all_gather | solution.py:161
  602.6 22.4 %reduce_sum.18 = bf16[32,32768]{1,0:T(8,128)(2,1)} reduce(f32[16,32,32768]{2,1,0:T(8,128)} %bitcast.17, f32[]{:T(128)} %constant.223.clone.1), dimensions={0}, to_apply=%region_2.3 | reduce | flops 15728640 | bytes 69206016 | tf_op jit(solution)/shard_map/reduce_sum | solution.py:161
  625.1 2.3 copy.58
  627.4 2.7 fusion.55
  630.1 4.0 fusion.56
  634.2 4.2 convolution_subtract_fusion
  638.4 6.8 copy.35
  645.2 5.7 convolution_add_fusion
  650.9 6.9 copy.36
  657.9 9.8 %fusion.54 = bf16[32,2,64,16,32]{2,4,3,0,1:T(8,128)(2,1)} fusion(f32[32,1,64,16,32]{2,4,3,0,1:T(8,128)} %bitcast.142, f32[32,1,64,16,32]{2,4,3,0,1:T(8,128)} %bitcast.141), kind=kLoop, calls=%fused_computation.97 | loop fusion | flops 6291456 | bytes 12582912 | tf_op jit(solution)/shard_map/convert_element_type | solution.py:108
  667.7 73.2 %while.28 = (s32[]{:T(128)}, f32[16,64,2048]{2,1,0:T(8,128)}, bf16[32,2,64,16,32]{2,4,3,0,1:T(8,128)(2,1)}, s32[]{:T(128)}, s32[]{:T(128)}, /*index=5*/s32[]{:T(128)}, s32[]{:T(128)}, s32[]{:T(128)}) while((s32[]{:T(128)}, f32[16,64,2048]{2,1,0:T(8,128)}, bf16[32,2,64,16,32]{2,4,3,0,1:T(8,128)(2,1)}, s32[]{:T(128)}, s32[]{:T(128)}, ...), condition=%wide.region_4.5_spmd.clone, body=%wide.region_3.4_spmd.clone.sunk | while | flops 2164789760 | bytes 23087320 | solution.py:127
  667.8 8.9 %cosine_convert_fusion.5 = (bf16[8,1,32,2048]{3,2,1,0:T(8,128)(2,1)S(1)}, bf16[8,1,32,2048]{3,2,1,0:T(8,128)(2,1)S(1)}) fusion(s32[2048]{0:T(1024)S(1)} %add_add_fusion.2, s32[8,32]{1,0:T(8,128)S(1)} %iota_add_fusion.4), kind=kLoop, calls=%fused_computation.85.clone.1 | loop fusion | flops 8912896 | bytes 2106368 | tf_op jit(solution)/shard_map/while/body/eval_jaxpr/convert_element_type | solution.py:44
  676.7 7.4 bitcast_add_fusion.2
  684.3 8.9 %cosine_convert_fusion.5 = (bf16[8,1,32,2048]{3,2,1,0:T(8,128)(2,1)S(1)}, bf16[8,1,32,2048]{3,2,1,0:T(8,128)(2,1)S(1)}) fusion(s32[2048]{0:T(1024)S(1)} %add_add_fusion.2, s32[8,32]{1,0:T(8,128)S(1)} %iota_add_fusion.4), kind=kLoop, calls=%fused_computation.85.clone.1 | loop fusion | flops 8912896 | bytes 2106368 | tf_op jit(solution)/shard_map/while/body/eval_jaxpr/convert_element_type | solution.py:44
  693.2 9.9 %bitcast_add_fusion.2 = f32[16,64,2048]{2,1,0:T(8,128)} fusion(f32[16,64,2048]{2,1,0:T(8,128)} %get-tuple-element.474, pred[]{:T(512)S(6)} %compare.19, bf16[8,1,32,2048]{3,2,1,0:T(8,128)(2,1)S(1)} %get-tuple-element.430, bf16[8,1,32,2048]{3,2,1,0:T(8,128)(2,1)S(1)} %get-tuple-element.431, bf16[32,2,64,16,32]{2,4,3,0,1:T(8,128)(2,1)} %get-tuple-element.483, ...), kind=kOutput, calls=%fused_computation.71.clone.1 | convolution fusion | flops 2155872256 | bytes 20971524 | tf_op jit(solution)/shard_map/while/body/eval_jaxpr/grycv,grvx->cyx/dot_general | solution.py:123
  703.2 8.9 %cosine_convert_fusion.5 = (bf16[8,1,32,2048]{3,2,1,0:T(8,128)(2,1)S(1)}, bf16[8,1,32,2048]{3,2,1,0:T(8,128)(2,1)S(1)}) fusion(s32[2048]{0:T(1024)S(1)} %add_add_fusion.2, s32[8,32]{1,0:T(8,128)S(1)} %iota_add_fusion.4), kind=kLoop, calls=%fused_computation.85.clone.1 | loop fusion | flops 8912896 | bytes 2106368 | tf_op jit(solution)/shard_map/while/body/eval_jaxpr/convert_element_type | solution.py:44
  712.1 9.9 %bitcast_add_fusion.2 = f32[16,64,2048]{2,1,0:T(8,128)} fusion(f32[16,64,2048]{2,1,0:T(8,128)} %get-tuple-element.474, pred[]{:T(512)S(6)} %compare.19, bf16[8,1,32,2048]{3,2,1,0:T(8,128)(2,1)S(1)} %get-tuple-element.430, bf16[8,1,32,2048]{3,2,1,0:T(8,128)(2,1)S(1)} %get-tuple-element.431, bf16[32,2,64,16,32]{2,4,3,0,1:T(8,128)(2,1)} %get-tuple-element.483, ...), kind=kOutput, calls=%fused_computation.71.clone.1 | convolution fusion | flops 2155872256 | bytes 20971524 | tf_op jit(solution)/shard_map/while/body/eval_jaxpr/grycv,grvx->cyx/dot_general | solution.py:123
  722.1 8.9 %cosine_convert_fusion.5 = (bf16[8,1,32,2048]{3,2,1,0:T(8,128)(2,1)S(1)}, bf16[8,1,32,2048]{3,2,1,0:T(8,128)(2,1)S(1)}) fusion(s32[2048]{0:T(1024)S(1)} %add_add_fusion.2, s32[8,32]{1,0:T(8,128)S(1)} %iota_add_fusion.4), kind=kLoop, calls=%fused_computation.85.clone.1 | loop fusion | flops 8912896 | bytes 2106368 | tf_op jit(solution)/shard_map/while/body/eval_jaxpr/convert_element_type | solution.py:44
  731.0 9.9 %bitcast_add_fusion.2 = f32[16,64,2048]{2,1,0:T(8,128)} fusion(f32[16,64,2048]{2,1,0:T(8,128)} %get-tuple-element.474, pred[]{:T(512)S(6)} %compare.19, bf16[8,1,32,2048]{3,2,1,0:T(8,128)(2,1)S(1)} %get-tuple-element.430, bf16[8,1,32,2048]{3,2,1,0:T(8,128)(2,1)S(1)} %get-tuple-element.431, bf16[32,2,64,16,32]{2,4,3,0,1:T(8,128)(2,1)} %get-tuple-element.483, ...), kind=kOutput, calls=%fused_computation.71.clone.1 | convolution fusion | flops 2155872256 | bytes 20971524 | tf_op jit(solution)/shard_map/while/body/eval_jaxpr/grycv,grvx->cyx/dot_general | solution.py:123
  742.0 3.4 collective-permute-start
  745.4 3.8 slice.85
  749.2 8.4 %collective-permute-done = f32[16,64,128]{2,1,0:T(8,128)S(1)} collective-permute-done((f32[16,64,128]{2,1,0:T(8,128)S(1)}, f32[16,64,128]{2,1,0:T(8,128)S(1)}, u32[]{:S(2)}, u32[]{:S(2)}) %collective-permute-start) | collective-permute-done | bytes 524320 | tf_op jit(solution)/shard_map/ppermute | solution.py:18
  758.7 4.6 pad_maximum_fusion
  (199 shorter events, 77.3 us)
Async XLA Ops:
  6.5 228.7 %copy-start = (s32[16,32]{1,0:T(8,128)S(1)}, s32[16,32]{1,0:T(8,128)}, u32[]{:S(2)}) copy-start(s32[16,32]{1,0:T(8,128)} %param.16) | copy-start | bytes 6148
  6.5 4.7 copy-start.2
  6.5 31.8 %copy-start.1 = (bf16[32,2,8]{0,2,1:T(8,128)(2,1)S(1)}, bf16[32,2,8]{0,2,1:T(8,128)(2,1)}, u32[]{:S(2)}) copy-start(bf16[32,2,8]{0,2,1:T(8,128)(2,1)} %param.12) | copy-start | bytes 3076
  6.5 31.8 %all-to-all-start = ((bf16[32,8,1,4096]{3,1,2,0:T(8,128)(2,1)}), bf16[32,8,1,4096]{3,1,2,0:T(8,128)(2,1)S(1)}, u32[]{:S(2)}, u32[]{:S(2)}) async-start(bf16[32,8,1,4096]{3,1,2,0:T(8,128)(2,1)} %param.11), calls=%async_computation | async-start | bytes 4194304 | tf_op jit(solution)/shard_map/all_to_all | solution.py:133
  11.1 591.5 %all-gather.3.cloned.1.call-start = ((), (), s32[]{:S(2)}) async-start(), calls=%async_computation.1 | async-start | bytes 71303168 | tf_op jit(solution)/shard_map/all_gather | solution.py:161
  233.4 0.7 copy-start.3
  742.0 15.6 %collective-permute-start = (f32[16,64,128]{2,1,0:T(8,128)S(1)}, f32[16,64,128]{2,1,0:T(8,128)S(1)}, u32[]{:S(2)}, u32[]{:S(2)}) collective-permute-start(f32[16,64,128]{2,1,0:T(8,128)S(1)} %slice_multiply_fusion), channel_id=1, source_target_pairs={{0,1},{1,2},{2,3},{3,4},{4,5},{5,6},{6,7},{7,8},{8,9},{9,10},{10,1... | collective-permute-start | bytes 1572872 | tf_op jit(solution)/shard_map/ppermute | solution.py:18
Sparse Core Ops, SparseCore 0:
  233.5 369.0 all-gather.2
